TPU v7x, 512 devices: a whole 4x4x16 slice. The times are simulated.
512 devices in a mesh: expert: 16 (over z), shard: 32 (over y, x, core).
Axes of the slice: x: 4, y: 4, z: 16, core: 2. Of those that a mesh axis runs over, the one named last changes fastest.
Arguments:
- tokens: bfloat16 [384, 6144], P('expert', 'shard'), may hold values from -6 to 6
- routes: int32 [384, 2], P('expert'), may hold values from 0 to 7, all different within a row; in each aligned block of 24 rows (0 to 23, 24 to 47, ...) at most 12 rows name the same one
- w_router: bfloat16 [6144, 8], replicated, may hold values from -0.078125 to 0.078125
- w_gate: bfloat16 [6144, 65536], P(None, ('expert', 'shard')), may hold values from -0.078125 to 0.078125
- w_up: bfloat16 [6144, 65536], P(None, ('expert', 'shard')), may hold values from -0.078125 to 0.078125
- w_down: bfloat16 [65536, 6144], P(('expert', 'shard')), may hold values from -0.25 to 0.25
Outputs:
- mixed: bfloat16 [384, 6144], P('expert', 'shard')
Inputs may be any that keep to these rules, and one draw needn't show every extreme that they name: `routes`: the two experts of a row differ; within each aligned block of 24 rows no expert is named more than 24 / 2 times, and some expert is named exactly that often.
All inputs are finite; a program needn't handle non-finite values.
Results may differ from a plain program's by a relative error of at most 0.017.
Values may be sent and summed in bfloat16 or wider, within the bound.
No kernel may reach another device: no remote copies, remote signals or barrier semaphores. Data moves between devices by JAX's collectives and lax.ppermute only.
A program may use at most 128 MiB of HBM per device.

v0:
```python
import jax
import jax.numpy as jnp
from jax import lax
from jax.sharding import PartitionSpec as P

FF_W = 8192


def sent_to_all(value, axis):
    peers = lax.axis_size(axis)
    return lax.all_to_all(
        jnp.broadcast_to(value[None], (peers, *value.shape)), axis, 0, 0, tiled=True
    )


def of_everyone(value, axis):
    everything = sent_to_all(value, axis)
    return jnp.sum(everything, axis=0)


def joined_along(blocks, dim):
    blocks = jnp.moveaxis(blocks, 0, dim)
    dims = blocks.shape
    return blocks.reshape(*dims[:dim], dims[dim] * dims[dim + 1], *dims[dim + 2 :])


def gather_directly(value, axis, dim):
    return joined_along(sent_to_all(value, axis), dim)


def cut_along(value, dim, peers):
    before, after = (value.shape[:dim], value.shape[dim + 1 :])
    return jnp.moveaxis(value.reshape(*before, peers, -1, *after), dim, 0)


def sum_at_owner(value, axis, dim):
    blocks = cut_along(value, dim, lax.axis_size(axis))
    arrived = lax.all_to_all(blocks, axis, split_axis=0, concat_axis=0, tiled=True)
    return arrived.astype(jnp.float32).sum(axis=0)


def local(tokens, routes, w_router, w_gate, w_up, w_down):
    tok_dev, dpiece = tokens.shape
    experts = w_router.shape[1]
    capacity = tok_dev // 2
    groups = lax.axis_size("expert")
    shards = lax.axis_size("shard")
    repeat = max(1, groups // experts)
    per_group = max(1, experts // groups)
    width = w_gate.shape[1]
    group_idx = lax.axis_index("expert")
    shard_idx = lax.axis_index("shard")
    expert_here = (group_idx * shards + shard_idx) * width // FF_W
    local_k = expert_here % per_group
    flat = routes.reshape(-1)
    onehot = (flat[:, None] == jnp.arange(experts)[None, :]).astype(jnp.int32)
    rank = jnp.cumsum(onehot, axis=0) - onehot
    slot = jnp.sum(rank * onehot, axis=1)
    target = flat * capacity + slot
    place = (target[:, None] == jnp.arange(experts * capacity)[None, :]).reshape(
        tok_dev, 2, experts * capacity
    )
    dispatch = jnp.any(place, axis=1).T.astype(jnp.bfloat16)
    rows_total = groups * capacity
    router_piece = lax.dynamic_slice_in_dim(w_router, shard_idx * dpiece, dpiece, 0)
    logits = of_everyone(jnp.dot(tokens, router_piece, preferred_element_type=jnp.float32), "shard")
    bucket = jnp.dot(dispatch, tokens, preferred_element_type=jnp.float32).astype(jnp.bfloat16)
    spread = jnp.repeat(bucket.reshape(experts, capacity, -1), repeat, axis=0)
    arrived = lax.all_to_all(
        spread.reshape(groups, per_group, capacity, -1),
        "expert",
        split_axis=0,
        concat_axis=0,
        tiled=True,
    )
    piece = gather_directly(arrived, "shard", 3)
    count = piece.shape[3]
    chosen = lax.dynamic_index_in_dim(piece, local_k, 1, keepdims=False).reshape(rows_total, count)
    gate = jnp.dot(chosen, w_gate, preferred_element_type=jnp.float32)
    up = jnp.dot(chosen, w_up, preferred_element_type=jnp.float32)
    hidden = (jax.nn.silu(gate) * up).astype(jnp.bfloat16)
    partial_out = jnp.dot(hidden, w_down, preferred_element_type=jnp.float32)
    keep = jnp.arange(per_group) == local_k
    term = jnp.where(keep[None, :, None, None], partial_out.reshape(groups, 1, capacity, -1), 0.0)
    shares = sum_at_owner(term.astype(jnp.bfloat16), "shard", 3)
    back = lax.all_to_all(
        shares.astype(jnp.bfloat16), "expert", split_axis=0, concat_axis=0, tiled=True
    )
    expert_out = jnp.sum(
        back.astype(jnp.float32).reshape(experts, repeat, capacity, dpiece), axis=1
    )
    expert_out = expert_out.reshape(experts * capacity, dpiece)
    picks = jnp.sum(
        jnp.where(
            routes[:, :, None] == jnp.arange(experts)[None, None, :], logits[:, None, :], 0.0
        ),
        axis=2,
    )
    first = 1.0 / (1.0 + jnp.exp(picks[:, 1] - picks[:, 0]))
    second = 1.0 / (1.0 + jnp.exp(picks[:, 0] - picks[:, 1]))
    weights = jnp.stack([first, second], axis=1)
    combine = jnp.sum(jnp.where(place, weights[:, :, None], 0.0), axis=1)
    mixed = jnp.dot(
        combine, expert_out, precision=lax.Precision.HIGHEST, preferred_element_type=jnp.float32
    )
    return mixed.astype(jnp.bfloat16)


def solution(mesh):
    return jax.shard_map(
        local,
        mesh=mesh,
        in_specs=(
            P("expert", "shard"),
            P("expert", None),
            P(),
            P(None, ("expert", "shard")),
            P(None, ("expert", "shard")),
            P(("expert", "shard"), None),
        ),
        out_specs=P("expert", "shard"),
        check_vma=False,
    )
```

profile of v0, /device:TPU:32, one launch (start us, length us, event | category | flops | bytes accessed | tf_op | source)
XLA Modules:
  0.0 189.0 jit_solution(6360991764029700150)
XLA Ops:
  0.0 0.0 copy-start
  0.0 0.9 copy.51
  0.9 0.1 eq.23
  1.0 0.1 fusion.8
  1.1 0.1 reduce_window_sum.11
  1.1 0.2 select_reduce_fusion.1
  1.3 0.1 reduce_sum.62
  1.4 0.1 copy.52
  1.5 0.7 multiply_add_fusion
  2.2 0.1 fusion.7
  2.3 0.9 convolution_convert_fusion.1
  3.2 29.2 %all_to_all.25 = bf16[16,1,12,192]{3,2,1,0:T(8,128)(2,1)S(1)} all-to-all(bf16[16,1,12,192]{3,2,1,0:T(8,128)(2,1)S(1)} %bitcast.34), channel_id=1, replica_groups=mesh['expert'=16,'shard'=32] {'expert'}, dimensions={0} | all-to-all | bytes 147456 | tf_op jit(solution)/shard_map/all_to_all | solution.py:69
  32.5 2.1 %broadcast_in_dim.64 = bf16[32,16,1,12,192]{4,1,3,2,0:T(8,128)(2,1)} broadcast(bf16[16,12,192]{2,0,1:T(8,128)(2,1)S(1)} %copy.53), dimensions={1,3,4} | broadcast | bytes 2433024 | tf_op jit(solution)/shard_map/broadcast_in_dim | solution.py:12
  34.5 0.0 copy-start.2
  34.5 7.6 %all-to-all-start.2 = ((bf16[32,16,1,12,192]{4,1,3,2,0:T(8,128)(2,1)}), bf16[32,16,1,12,192]{4,1,3,2,0:T(8,128)(2,1)}, u32[]{:S(2)}, u32[]{:S(2)}) async-start(bf16[32,16,1,12,192]{4,1,3,2,0:T(8,128)(2,1)} %broadcast_in_dim.64), calls=%async_computation.2 | async-start | bytes 6291456 | tf_op jit(solution)/shard_map/all_to_all | solution.py:11
  42.1 0.0 copy-done.2
  42.1 0.9 convolution_bitcast_fusion
  43.0 0.7 reshape.73
  43.8 40.1 %all-to-all-done.2 = bf16[32,16,1,12,192]{4,1,3,2,0:T(8,128)(2,1)} async-done(((bf16[32,16,1,12,192]{4,1,3,2,0:T(8,128)(2,1)}), bf16[32,16,1,12,192]{4,1,3,2,0:T(8,128)(2,1)}, u32[]{:S(2)}, u32[]{:S(2)}) %all-to-all-start.2) | async-done | bytes 2359328 | tf_op jit(solution)/shard_map/all_to_all | solution.py:11
  83.9 3.8 %all-to-all-start = ((f32[32,1,192]{2,1,0:T(1,128)}), f32[32,1,192]{2,1,0:T(1,128)S(1)}, u32[]{:S(2)}, u32[]{:S(2)}) async-start(f32[32,1,192]{2,1,0:T(1,128)} %reshape.73), calls=%async_computation | async-start | bytes 65536 | tf_op jit(solution)/shard_map/all_to_all | solution.py:11
  87.7 5.4 %copy.54 = bf16[16,1,12,32,192]{4,3,2,0,1:T(8,128)(2,1)} copy(bf16[16,1,12,32,192]{4,0,2,1,3:T(8,128)(2,1)} %bitcast.3) | data formatting | bytes 4718592 | tf_op jit(solution)/shard_map/transpose | solution.py:22
  93.0 0.0 copy-start.1
  93.0 6.3 %reshape.67 = bf16[192,6144]{1,0:T(8,128)(2,1)} reshape(bf16[16,1,12,32,192]{4,3,2,0,1:T(8,128)(2,1)} %copy.54) | data formatting | bytes 4718592 | tf_op jit(solution)/shard_map/reshape | solution.py:78
  99.4 0.0 copy-done.1
  99.4 2.4 %fusion.12 = f32[192,128]{1,0:T(8,128)S(1)} fusion(bf16[192,6144]{1,0:T(8,128)(2,1)} %reshape.67, bf16[6144,128]{1,0:T(8,128)(2,1)S(1)} %copy-done.1), kind=kOutput, calls=%fused_computation.31 | convolution fusion | flops 301989888 | bytes 4030464 | tf_op jit(solution)/shard_map/dot_general | solution.py:79
  101.8 0.0 copy-done
  101.8 5.0 %convolution_convert_fusion = bf16[192,6144]{1,0:T(8,128)(2,1)} fusion(bf16[128,6144]{1,0:T(8,128)(2,1)S(1)} %copy-done, bf16[192,6144]{1,0:T(8,128)(2,1)} %reshape.67, bf16[6144,128]{1,0:T(8,128)(2,1)} %param.10, f32[192,128]{1,0:T(8,128)S(1)} %fusion.12), kind=kOutput, calls=%fused_computation | convolution fusion | flops 605306880 | bytes 7962624 | tf_op jit(solution)/shard_map/dot_general | solution.py:82
  106.8 6.4 %convert_element_type.35 = bf16[16,1,12,32,192]{4,3,2,0,1:T(8,128)(2,1)} reshape(bf16[192,6144]{1,0:T(8,128)(2,1)} %convolution_convert_fusion) | data formatting | bytes 4718592 | tf_op jit(solution)/shard_map/convert_element_type | solution.py:85
  113.3 5.3 %copy.58 = bf16[16,1,12,32,192]{4,0,2,1,3:T(8,128)(2,1)} copy(bf16[16,1,12,32,192]{4,3,2,0,1:T(8,128)(2,1)} %convert_element_type.35) | data formatting | bytes 4718592 | tf_op jit(solution)/shard_map/convert_element_type | solution.py:85
  118.6 0.0 all-to-all-done
  118.6 0.0 copy-start.3
  118.6 7.6 %all-to-all-start.3 = ((bf16[32,16,1,12,192]{4,1,3,2,0:T(8,128)(2,1)}), bf16[32,16,1,12,192]{4,1,3,2,0:T(8,128)(2,1)}, u32[]{:S(2)}, u32[]{:S(2)}) async-start(bf16[32,16,1,12,192]{4,1,3,2,0:T(8,128)(2,1)} %bitcast.31), calls=%async_computation.3 | async-start | bytes 6291456 | tf_op jit(solution)/shard_map/all_to_all | solution.py:38
  126.2 0.5 broadcast.44
  126.7 0.7 reduce.2
  127.5 0.1 reshape.74
  127.6 0.0 copy-done.3
  127.6 40.4 %all-to-all-done.3 = bf16[32,16,1,12,192]{4,1,3,2,0:T(8,128)(2,1)} async-done(((bf16[32,16,1,12,192]{4,1,3,2,0:T(8,128)(2,1)}), bf16[32,16,1,12,192]{4,1,3,2,0:T(8,128)(2,1)}, u32[]{:S(2)}, u32[]{:S(2)}) %all-to-all-start.3) | async-done | bytes 2359328 | tf_op jit(solution)/shard_map/all_to_all | solution.py:38
  168.0 2.4 %reduce_sum.66 = bf16[16,12,192]{2,0,1:T(8,128)(2,1)S(1)} reduce(bf16[32,16,1,12,192]{4,1,3,2,0:T(8,128)(2,1)} %all-to-all-done.3, bf16[]{:T(256)} %constant.60.clone.1), dimensions={0,2}, to_apply=%region_6.7 | reduce | flops 1142784 | bytes 2433026 | tf_op jit(solution)/shard_map/reduce_sum | solution.py:39
  170.4 0.7 copy.56
  171.1 4.3 %all-to-all-start.4 = ((bf16[16,1,12,192]{3,2,1,0:T(8,128)(2,1)}), bf16[16,1,12,192]{3,2,1,0:T(8,128)(2,1)S(1)}, u32[]{:S(2)}, u32[]{:S(2)}) async-start(bf16[16,1,12,192]{3,2,1,0:T(8,128)(2,1)} %copy.56), calls=%async_computation.4 | async-start | bytes 262144 | tf_op jit(solution)/shard_map/all_to_all | solution.py:86
  175.4 0.1 select_reduce_fusion
  175.5 12.6 %all-to-all-done.4 = bf16[16,1,12,192]{3,2,1,0:T(8,128)(2,1)S(1)} async-done(((bf16[16,1,12,192]{3,2,1,0:T(8,128)(2,1)}), bf16[16,1,12,192]{3,2,1,0:T(8,128)(2,1)S(1)}, u32[]{:S(2)}, u32[]{:S(2)}) %all-to-all-start.4) | async-done | bytes 73760 | tf_op jit(solution)/shard_map/all_to_all | solution.py:86
  188.2 0.8 convolution_convert_fusion.2
  (10 shorter events, 0.2 us)
Async XLA Ops:
  0.0 101.8 %copy-start = (bf16[128,6144]{1,0:T(8,128)(2,1)S(1)}, bf16[128,6144]{1,0:T(8,128)(2,1)}, u32[]{:S(2)}) copy-start(bf16[128,6144]{1,0:T(8,128)(2,1)} %param.11) | copy-start | bytes 4718596
  34.5 7.6 %copy-start.2 = (bf16[24,192]{1,0:T(8,128)(2,1)S(1)}, bf16[24,192]{1,0:T(8,128)(2,1)}, u32[]{:S(2)}) copy-start(bf16[24,192]{1,0:T(8,128)(2,1)} %param.6) | copy-start | bytes 27652
  34.5 49.3 %all-to-all-start.2 = ((bf16[32,16,1,12,192]{4,1,3,2,0:T(8,128)(2,1)}), bf16[32,16,1,12,192]{4,1,3,2,0:T(8,128)(2,1)}, u32[]{:S(2)}, u32[]{:S(2)}) async-start(bf16[32,16,1,12,192]{4,1,3,2,0:T(8,128)(2,1)} %broadcast_in_dim.64), calls=%async_computation.2 | async-start | bytes 6291456 | tf_op jit(solution)/shard_map/all_to_all | solution.py:11
  83.9 34.7 %all-to-all-start = ((f32[32,1,192]{2,1,0:T(1,128)}), f32[32,1,192]{2,1,0:T(1,128)S(1)}, u32[]{:S(2)}, u32[]{:S(2)}) async-start(f32[32,1,192]{2,1,0:T(1,128)} %reshape.73), calls=%async_computation | async-start | bytes 65536 | tf_op jit(solution)/shard_map/all_to_all | solution.py:11
  93.0 6.3 %copy-start.1 = (bf16[6144,128]{1,0:T(8,128)(2,1)S(1)}, bf16[6144,128]{1,0:T(8,128)(2,1)}, u32[]{:S(2)}) copy-start(bf16[6144,128]{1,0:T(8,128)(2,1)} %param.9) | copy-start | bytes 4718596
  118.6 9.0 %copy-start.3 = (s32[24,2]{0,1:T(2,128)S(1)}, s32[24,2]{0,1:T(2,128)}, u32[]{:S(2)}) copy-start(s32[24,2]{0,1:T(2,128)} %param.7) | copy-start | bytes 580
  118.6 49.4 %all-to-all-start.3 = ((bf16[32,16,1,12,192]{4,1,3,2,0:T(8,128)(2,1)}), bf16[32,16,1,12,192]{4,1,3,2,0:T(8,128)(2,1)}, u32[]{:S(2)}, u32[]{:S(2)}) async-start(bf16[32,16,1,12,192]{4,1,3,2,0:T(8,128)(2,1)} %bitcast.31), calls=%async_computation.3 | async-start | bytes 6291456 | tf_op jit(solution)/shard_map/all_to_all | solution.py:38
  171.1 17.1 %all-to-all-start.4 = ((bf16[16,1,12,192]{3,2,1,0:T(8,128)(2,1)}), bf16[16,1,12,192]{3,2,1,0:T(8,128)(2,1)S(1)}, u32[]{:S(2)}, u32[]{:S(2)}) async-start(bf16[16,1,12,192]{3,2,1,0:T(8,128)(2,1)} %copy.56), calls=%async_computation.4 | async-start | bytes 262144 | tf_op jit(solution)/shard_map/all_to_all | solution.py:86
where the time goes:
time: 190 us; the launch traced here: 189 us
  waiting for transfers between devices  93.1 us (49%)
  blocking collectives  29.2 us (15%)
  local copies, waits for them, and re-layouts  28.8 us (15%)
  starting transfers between devices  23.3 us (12%)
  matrix products  10 us (5%)
  other arithmetic  4.44 us (2%)
    all_to_all x1, waiting for transfers between devices, sum_at_owner(): lax.all_to_all(blocks, axis, split_axis=0, concat_axis=0, tiled=True)  40.4 us
    all_to_all x2, waiting for transfers between devices, sent_to_all(): lax.all_to_all(jnp.broadcast_to(value[None], (peers, *value.shape)), axis...  40.1 us
    all_to_all x1, blocking collectives, local(): lax.all_to_all(spread.reshape(groups, per_group, capacity, -1), 'expert',...  29.2 us
    all_to_all x1, waiting for transfers between devices, local(): lax.all_to_all(shares.astype(jnp.bfloat16), 'expert', split_axis=0, conca...  12.6 us
    convert_element_type x2, local copies, waits for them, and re-layouts, local(): shares = sum_at_owner(term.astype(jnp.bfloat16), 'shard', 3)  11.8 us
    all_to_all x2, starting transfers between devices, sent_to_all(): lax.all_to_all(jnp.broadcast_to(value[None], (peers, *value.shape)), axis...  11.4 us
    all_to_all x1, starting transfers between devices, sum_at_owner(): lax.all_to_all(blocks, axis, split_axis=0, concat_axis=0, tiled=True)  7.63 us
    reshape x1, local copies, waits for them, and re-layouts, local(): lax.dynamic_index_in_dim(piece, local_k, 1, keepdims=False)  6.31 us
  transfers between devices with their start and end apart: 4, of which 3 were waited for; matrix products, arithmetic and copies ran while one was open for 18% of the time, Pallas kernels for 0%

commit v1 on v0

--- a/solution.py
+++ b/solution.py
@@ -4,6 +4,17 @@
 from jax.sharding import PartitionSpec as P
 
 FF_W = 8192
+
+
+def cut_along_2(value, dim, peers):
+    before, after = (value.shape[:dim], value.shape[dim + 1 :])
+    return jnp.moveaxis(value.reshape(*before, peers, -1, *after), dim, 0)
+
+
+def laid_out(parts, dim):
+    parts = jnp.moveaxis(parts, 0, dim)
+    lengths = parts.shape
+    return parts.reshape(*lengths[:dim], lengths[dim] * lengths[dim + 1], *lengths[dim + 2 :])
 
 
 def sent_to_all(value, axis):
@@ -66,13 +77,15 @@
     logits = of_everyone(jnp.dot(tokens, router_piece, preferred_element_type=jnp.float32), "shard")
     bucket = jnp.dot(dispatch, tokens, preferred_element_type=jnp.float32).astype(jnp.bfloat16)
     spread = jnp.repeat(bucket.reshape(experts, capacity, -1), repeat, axis=0)
-    arrived = lax.all_to_all(
-        spread.reshape(groups, per_group, capacity, -1),
-        "expert",
-        split_axis=0,
-        concat_axis=0,
-        tiled=True,
-    )
+    x = spread.reshape(groups, per_group, capacity, -1)
+    size, position = (lax.axis_size("expert"), lax.axis_index("expert"))
+    pieces = cut_along_2(x, 0, size)
+    finished = [pieces[position]]
+    for step in range(1, size):
+        sent = pieces[position ^ step]
+        finished.append(lax.ppermute(sent, "expert", [(i, i ^ step) for i in range(size)]))
+    pieces = jnp.stack(finished)[position ^ jnp.arange(size)]
+    arrived = laid_out(pieces, 0)
     piece = gather_directly(arrived, "shard", 3)
     count = piece.shape[3]
     chosen = lax.dynamic_index_in_dim(piece, local_k, 1, keepdims=False).reshape(rows_total, count)

time: 190 us -> 254 us (1.34)
  starting transfers between devices: 23.3 us -> 110 us
  blocking collectives: 29.2 us -> 0 us
  waiting for transfers between devices: 93.1 us -> 98.3 us
    ppermute x0 -> x15, starting transfers between devices: none -> 81.3 us  [local(): lax.ppermute(sent, 'expert', [(i, i ^ step) for i in range(size)])]
    all_to_all x1 -> x0, blocking collectives: 29.2 us -> none  [local(): lax.all_to_all(spread.reshape(groups, per_group, capacity, -1), 'expert',...]
    all_to_all x1, starting transfers between devices: 4.33 us -> 9.78 us  [local(): lax.all_to_all(shares.astype(jnp.bfloat16), 'expert', split_axis=0, conca...]
    ppermute x0 -> x15, waiting for transfers between devices: none -> 5.21 us  [local(): lax.ppermute(sent, 'expert', [(i, i ^ step) for i in range(size)])]
  transfers between devices with their start and end apart: 4 -> 19, of which waited for: 3 -> 4; matrix products, arithmetic and copies ran while one was open for 18% -> 13% of each run, Pallas kernels for 0% -> 0%
where the time goes in v1:
time: 254 us; the launch traced here: 253 us
  starting transfers between devices  110 us (43%)
  waiting for transfers between devices  98.3 us (39%)
  local copies, waits for them, and re-layouts  29.4 us (12%)
  matrix products  10 us (4%)
  other arithmetic  4.45 us (2%)
    ppermute x15, starting transfers between devices, local(): lax.ppermute(sent, 'expert', [(i, i ^ step) for i in range(size)])  81.3 us
    all_to_all x1, waiting for transfers between devices, sum_at_owner(): lax.all_to_all(blocks, axis, split_axis=0, concat_axis=0, tiled=True)  40.4 us
    all_to_all x2, waiting for transfers between devices, sent_to_all(): lax.all_to_all(jnp.broadcast_to(value[None], (peers, *value.shape)), axis...  40.1 us
    all_to_all x1, waiting for transfers between devices, local(): lax.all_to_all(shares.astype(jnp.bfloat16), 'expert', split_axis=0, conca...  12.6 us
    convert_element_type x2, local copies, waits for them, and re-layouts, local(): shares = sum_at_owner(term.astype(jnp.bfloat16), 'shard', 3)  11.7 us
    all_to_all x2, starting transfers between devices, sent_to_all(): lax.all_to_all(jnp.broadcast_to(value[None], (peers, *value.shape)), axis...  11.4 us
    all_to_all x1, starting transfers between devices, local(): lax.all_to_all(shares.astype(jnp.bfloat16), 'expert', split_axis=0, conca...  9.78 us
    all_to_all x1, starting transfers between devices, sum_at_owner(): lax.all_to_all(blocks, axis, split_axis=0, concat_axis=0, tiled=True)  7.63 us
  transfers between devices with their start and end apart: 19, of which 4 were waited for; matrix products, arithmetic and copies ran while one was open for 13% of the time, Pallas kernels for 0%

profile of v1, /device:TPU:32, one launch (start us, length us, event | category | flops | bytes accessed | tf_op | source)
XLA Modules:
  0.0 252.9 jit_solution(14032363248070942966)
XLA Ops:
  0.0 0.9 copy.59
  0.9 0.1 eq.23
  1.1 0.2 select_reduce_fusion.1
  1.3 0.1 reduce_sum.62
  1.5 0.7 multiply_add_fusion
  2.2 0.1 fusion.7
  2.3 0.9 convolution_convert_fusion.1
  3.3 0.1 dynamic-slice_bitcast_fusion
  3.4 7.4 %collective-permute-start = (bf16[1,1,12,192]{3,2,1,0:T(8,128)(2,1)S(1)}, bf16[1,1,12,192]{3,2,1,0:T(8,128)(2,1)S(1)}, u32[]{:S(2)}, u32[]{:S(2)}) collective-permute-start(bf16[1,1,12,192]{3,2,1,0:T(8,128)(2,1)S(1)} %get-tuple-element.19), channel_id=1, source_target_pairs={{0,32},{32,0},{64,96},{96,64},{128,160},{160,128},{192,224},{224,1... | collective-permute-start | bytes 13832 | tf_op jit(solution)/shard_map/ppermute | solution.py:86
  10.8 1.9 collective-permute-start.1
  12.7 3.4 %collective-permute-start.2 = (bf16[1,1,12,192]{3,2,1,0:T(8,128)(2,1)S(1)}, bf16[1,1,12,192]{3,2,1,0:T(8,128)(2,1)S(1)}, u32[]{:S(2)}, u32[]{:S(2)}) collective-permute-start(bf16[1,1,12,192]{3,2,1,0:T(8,128)(2,1)S(1)} %get-tuple-element.17), channel_id=1, source_target_pairs={{0,96},{32,64},{64,32},{96,0},{128,224},{160,192},{192,160},{224,1... | collective-permute-start | bytes 13832 | tf_op jit(solution)/shard_map/ppermute | solution.py:86
  16.1 6.0 %collective-permute-start.3 = (bf16[1,1,12,192]{3,2,1,0:T(8,128)(2,1)S(1)}, bf16[1,1,12,192]{3,2,1,0:T(8,128)(2,1)S(1)}, u32[]{:S(2)}, u32[]{:S(2)}) collective-permute-start(bf16[1,1,12,192]{3,2,1,0:T(8,128)(2,1)S(1)} %get-tuple-element.16), channel_id=1, source_target_pairs={{0,128},{32,160},{64,192},{96,224},{128,0},{160,32},{192,64},{224,... | collective-permute-start | bytes 13832 | tf_op jit(solution)/shard_map/ppermute | solution.py:86
  22.1 5.2 %collective-permute-start.4 = (bf16[1,1,12,192]{3,2,1,0:T(8,128)(2,1)S(1)}, bf16[1,1,12,192]{3,2,1,0:T(8,128)(2,1)S(1)}, u32[]{:S(2)}, u32[]{:S(2)}) collective-permute-start(bf16[1,1,12,192]{3,2,1,0:T(8,128)(2,1)S(1)} %get-tuple-element.15), channel_id=1, source_target_pairs={{0,160},{32,128},{64,224},{96,192},{128,32},{160,0},{192,96},{224,... | collective-permute-start | bytes 13832 | tf_op jit(solution)/shard_map/ppermute | solution.py:86
  27.4 6.4 %collective-permute-start.5 = (bf16[1,1,12,192]{3,2,1,0:T(8,128)(2,1)S(1)}, bf16[1,1,12,192]{3,2,1,0:T(8,128)(2,1)S(1)}, u32[]{:S(2)}, u32[]{:S(2)}) collective-permute-start(bf16[1,1,12,192]{3,2,1,0:T(8,128)(2,1)S(1)} %get-tuple-element.14), channel_id=1, source_target_pairs={{0,192},{32,224},{64,128},{96,160},{128,64},{160,96},{192,0},{224,... | collective-permute-start | bytes 13832 | tf_op jit(solution)/shard_map/ppermute | solution.py:86
  33.8 3.7 %collective-permute-start.6 = (bf16[1,1,12,192]{3,2,1,0:T(8,128)(2,1)S(1)}, bf16[1,1,12,192]{3,2,1,0:T(8,128)(2,1)S(1)}, u32[]{:S(2)}, u32[]{:S(2)}) collective-permute-start(bf16[1,1,12,192]{3,2,1,0:T(8,128)(2,1)S(1)} %get-tuple-element.13), channel_id=1, source_target_pairs={{0,224},{32,192},{64,160},{96,128},{128,96},{160,64},{192,32},{224... | collective-permute-start | bytes 13832 | tf_op jit(solution)/shard_map/ppermute | solution.py:86
  37.5 11.4 %collective-permute-start.7 = (bf16[1,1,12,192]{3,2,1,0:T(8,128)(2,1)S(1)}, bf16[1,1,12,192]{3,2,1,0:T(8,128)(2,1)S(1)}, u32[]{:S(2)}, u32[]{:S(2)}) collective-permute-start(bf16[1,1,12,192]{3,2,1,0:T(8,128)(2,1)S(1)} %get-tuple-element.12), channel_id=1, source_target_pairs={{0,256},{32,288},{64,320},{96,352},{128,384},{160,416},{192,448},{... | collective-permute-start | bytes 13832 | tf_op jit(solution)/shard_map/ppermute | solution.py:86
  48.9 4.7 %collective-permute-start.8 = (bf16[1,1,12,192]{3,2,1,0:T(8,128)(2,1)S(1)}, bf16[1,1,12,192]{3,2,1,0:T(8,128)(2,1)S(1)}, u32[]{:S(2)}, u32[]{:S(2)}) collective-permute-start(bf16[1,1,12,192]{3,2,1,0:T(8,128)(2,1)S(1)} %get-tuple-element.11), channel_id=1, source_target_pairs={{0,288},{32,256},{64,352},{96,320},{128,416},{160,384},{192,480},{... | collective-permute-start | bytes 13832 | tf_op jit(solution)/shard_map/ppermute | solution.py:86
  53.6 5.0 %collective-permute-start.9 = (bf16[1,1,12,192]{3,2,1,0:T(8,128)(2,1)S(1)}, bf16[1,1,12,192]{3,2,1,0:T(8,128)(2,1)S(1)}, u32[]{:S(2)}, u32[]{:S(2)}) collective-permute-start(bf16[1,1,12,192]{3,2,1,0:T(8,128)(2,1)S(1)} %get-tuple-element.10), channel_id=1, source_target_pairs={{0,320},{32,352},{64,256},{96,288},{128,448},{160,480},{192,384},{... | collective-permute-start | bytes 13832 | tf_op jit(solution)/shard_map/ppermute | solution.py:86
  58.6 6.4 %collective-permute-start.10 = (bf16[1,1,12,192]{3,2,1,0:T(8,128)(2,1)S(1)}, bf16[1,1,12,192]{3,2,1,0:T(8,128)(2,1)S(1)}, u32[]{:S(2)}, u32[]{:S(2)}) collective-permute-start(bf16[1,1,12,192]{3,2,1,0:T(8,128)(2,1)S(1)} %get-tuple-element.9), channel_id=1, source_target_pairs={{0,352},{32,320},{64,288},{96,256},{128,480},{160,448},{192,416},{... | collective-permute-start | bytes 13832 | tf_op jit(solution)/shard_map/ppermute | solution.py:86
  65.0 5.0 %collective-permute-start.11 = (bf16[1,1,12,192]{3,2,1,0:T(8,128)(2,1)S(1)}, bf16[1,1,12,192]{3,2,1,0:T(8,128)(2,1)S(1)}, u32[]{:S(2)}, u32[]{:S(2)}) collective-permute-start(bf16[1,1,12,192]{3,2,1,0:T(8,128)(2,1)S(1)} %get-tuple-element.8), channel_id=1, source_target_pairs={{0,384},{32,416},{64,448},{96,480},{128,256},{160,288},{192,320},{... | collective-permute-start | bytes 13832 | tf_op jit(solution)/shard_map/ppermute | solution.py:86
  70.1 6.1 %collective-permute-start.12 = (bf16[1,1,12,192]{3,2,1,0:T(8,128)(2,1)S(1)}, bf16[1,1,12,192]{3,2,1,0:T(8,128)(2,1)S(1)}, u32[]{:S(2)}, u32[]{:S(2)}) collective-permute-start(bf16[1,1,12,192]{3,2,1,0:T(8,128)(2,1)S(1)} %get-tuple-element.7), channel_id=1, source_target_pairs={{0,416},{32,384},{64,480},{96,448},{128,288},{160,256},{192,352},{... | collective-permute-start | bytes 13832 | tf_op jit(solution)/shard_map/ppermute | solution.py:86
  76.2 5.6 %collective-permute-start.13 = (bf16[1,1,12,192]{3,2,1,0:T(8,128)(2,1)S(1)}, bf16[1,1,12,192]{3,2,1,0:T(8,128)(2,1)S(1)}, u32[]{:S(2)}, u32[]{:S(2)}) collective-permute-start(bf16[1,1,12,192]{3,2,1,0:T(8,128)(2,1)S(1)} %get-tuple-element.6), channel_id=1, source_target_pairs={{0,448},{32,480},{64,384},{96,416},{128,320},{160,352},{192,256},{... | collective-permute-start | bytes 13832 | tf_op jit(solution)/shard_map/ppermute | solution.py:86
  81.8 3.3 %collective-permute-start.14 = (bf16[1,1,12,192]{3,2,1,0:T(8,128)(2,1)S(1)}, bf16[1,1,12,192]{3,2,1,0:T(8,128)(2,1)S(1)}, u32[]{:S(2)}, u32[]{:S(2)}) collective-permute-start(bf16[1,1,12,192]{3,2,1,0:T(8,128)(2,1)S(1)} %get-tuple-element.5), channel_id=1, source_target_pairs={{0,480},{32,448},{64,416},{96,384},{128,352},{160,320},{192,288},{... | collective-permute-start | bytes 13832 | tf_op jit(solution)/shard_map/ppermute | solution.py:86
  85.2 5.2 %collective-permute-done.14 = bf16[1,1,12,192]{3,2,1,0:T(8,128)(2,1)S(1)} collective-permute-done((bf16[1,1,12,192]{3,2,1,0:T(8,128)(2,1)S(1)}, bf16[1,1,12,192]{3,2,1,0:T(8,128)(2,1)S(1)}, u32[]{:S(2)}, u32[]{:S(2)}) %collective-permute-start.14) | collective-permute-done | bytes 4640 | tf_op jit(solution)/shard_map/ppermute | solution.py:86
  90.4 0.6 gather_fusion
  91.0 2.0 broadcast_in_dim.64
  93.0 7.6 %all-to-all-start.1 = ((bf16[32,16,1,12,192]{4,1,3,2,0:T(8,128)(2,1)}), bf16[32,16,1,12,192]{4,1,3,2,0:T(8,128)(2,1)}, u32[]{:S(2)}, u32[]{:S(2)}) async-start(bf16[32,16,1,12,192]{4,1,3,2,0:T(8,128)(2,1)} %broadcast_in_dim.64), calls=%async_computation.1 | async-start | bytes 6291456 | tf_op jit(solution)/shard_map/all_to_all | solution.py:22
  100.6 0.9 convolution_bitcast_fusion
  101.5 0.8 reshape.104
  102.3 40.1 %all-to-all-done.1 = bf16[32,16,1,12,192]{4,1,3,2,0:T(8,128)(2,1)} async-done(((bf16[32,16,1,12,192]{4,1,3,2,0:T(8,128)(2,1)}), bf16[32,16,1,12,192]{4,1,3,2,0:T(8,128)(2,1)}, u32[]{:S(2)}, u32[]{:S(2)}) %all-to-all-start.1) | async-done | bytes 2359328 | tf_op jit(solution)/shard_map/all_to_all | solution.py:22
  142.4 3.8 %all-to-all-start = ((f32[32,1,192]{2,1,0:T(1,128)}), f32[32,1,192]{2,1,0:T(1,128)S(1)}, u32[]{:S(2)}, u32[]{:S(2)}) async-start(f32[32,1,192]{2,1,0:T(1,128)} %reshape.104), calls=%async_computation | async-start | bytes 65536 | tf_op jit(solution)/shard_map/all_to_all | solution.py:22
  146.2 5.3 %copy.62 = bf16[16,1,12,32,192]{4,3,2,0,1:T(8,128)(2,1)} copy(bf16[16,1,12,32,192]{4,0,2,1,3:T(8,128)(2,1)} %bitcast.34) | data formatting | bytes 4718592 | tf_op jit(solution)/shard_map/transpose | solution.py:33
  151.5 6.3 %reshape.83 = bf16[192,6144]{1,0:T(8,128)(2,1)} reshape(bf16[16,1,12,32,192]{4,3,2,0,1:T(8,128)(2,1)} %copy.62) | data formatting | bytes 4718592 | tf_op jit(solution)/shard_map/reshape | solution.py:91
  157.8 2.4 fusion.11
  160.3 5.0 %convolution_convert_fusion = bf16[192,6144]{1,0:T(8,128)(2,1)} fusion(bf16[128,6144]{1,0:T(8,128)(2,1)S(1)} %copy-done, bf16[192,6144]{1,0:T(8,128)(2,1)} %reshape.83, bf16[6144,128]{1,0:T(8,128)(2,1)} %param.10, f32[192,128]{1,0:T(8,128)S(1)} %fusion.11), kind=kOutput, calls=%fused_computation.1 | convolution fusion | flops 605306880 | bytes 7962624 | tf_op jit(solution)/shard_map/dot_general | solution.py:95
  165.3 6.4 %convert_element_type.35 = bf16[16,1,12,32,192]{4,3,2,0,1:T(8,128)(2,1)} reshape(bf16[192,6144]{1,0:T(8,128)(2,1)} %convolution_convert_fusion) | data formatting | bytes 4718592 | tf_op jit(solution)/shard_map/convert_element_type | solution.py:98
  171.7 5.3 %copy.66 = bf16[16,1,12,32,192]{4,0,2,1,3:T(8,128)(2,1)} copy(bf16[16,1,12,32,192]{4,3,2,0,1:T(8,128)(2,1)} %convert_element_type.35) | data formatting | bytes 4718592 | tf_op jit(solution)/shard_map/convert_element_type | solution.py:98
  177.0 7.6 %all-to-all-start.2 = ((bf16[32,16,1,12,192]{4,1,3,2,0:T(8,128)(2,1)}), bf16[32,16,1,12,192]{4,1,3,2,0:T(8,128)(2,1)}, u32[]{:S(2)}, u32[]{:S(2)}) async-start(bf16[32,16,1,12,192]{4,1,3,2,0:T(8,128)(2,1)} %bitcast.93), calls=%async_computation.2 | async-start | bytes 6291456 | tf_op jit(solution)/shard_map/all_to_all | solution.py:49
  184.7 0.5 broadcast.80
  185.2 0.7 reduce.2
  185.9 0.1 reshape.105
  186.1 40.4 %all-to-all-done.2 = bf16[32,16,1,12,192]{4,1,3,2,0:T(8,128)(2,1)} async-done(((bf16[32,16,1,12,192]{4,1,3,2,0:T(8,128)(2,1)}), bf16[32,16,1,12,192]{4,1,3,2,0:T(8,128)(2,1)}, u32[]{:S(2)}, u32[]{:S(2)}) %all-to-all-start.2) | async-done | bytes 2359328 | tf_op jit(solution)/shard_map/all_to_all | solution.py:49
  226.4 2.4 reduce_sum.66
  228.9 0.7 copy.64
  229.6 9.8 %all-to-all-start.3 = ((bf16[16,1,12,192]{3,2,1,0:T(8,128)(2,1)}), bf16[16,1,12,192]{3,2,1,0:T(8,128)(2,1)S(1)}, u32[]{:S(2)}, u32[]{:S(2)}) async-start(bf16[16,1,12,192]{3,2,1,0:T(8,128)(2,1)} %copy.64), calls=%async_computation.3 | async-start | bytes 262144 | tf_op jit(solution)/shard_map/all_to_all | solution.py:99
  239.4 0.1 select_reduce_fusion
  239.5 12.6 %all-to-all-done.3 = bf16[16,1,12,192]{3,2,1,0:T(8,128)(2,1)S(1)} async-done(((bf16[16,1,12,192]{3,2,1,0:T(8,128)(2,1)}), bf16[16,1,12,192]{3,2,1,0:T(8,128)(2,1)S(1)}, u32[]{:S(2)}, u32[]{:S(2)}) %all-to-all-start.3) | async-done | bytes 73760 | tf_op jit(solution)/shard_map/all_to_all | solution.py:99
  252.1 0.8 convolution_convert_fusion.2
  (53 shorter events, 0.5 us)
Async XLA Ops:
  0.0 160.2 %copy-start = (bf16[128,6144]{1,0:T(8,128)(2,1)S(1)}, bf16[128,6144]{1,0:T(8,128)(2,1)}, u32[]{:S(2)}) copy-start(bf16[128,6144]{1,0:T(8,128)(2,1)} %param.11) | copy-start | bytes 4718596
  3.4 24.0 %collective-permute-start = (bf16[1,1,12,192]{3,2,1,0:T(8,128)(2,1)S(1)}, bf16[1,1,12,192]{3,2,1,0:T(8,128)(2,1)S(1)}, u32[]{:S(2)}, u32[]{:S(2)}) collective-permute-start(bf16[1,1,12,192]{3,2,1,0:T(8,128)(2,1)S(1)} %get-tuple-element.19), channel_id=1, source_target_pairs={{0,32},{32,0},{64,96},{96,64},{128,160},{160,128},{192,224},{224,1... | collective-permute-start | bytes 13832 | tf_op jit(solution)/shard_map/ppermute | solution.py:86
  10.8 23.0 %collective-permute-start.1 = (bf16[1,1,12,192]{3,2,1,0:T(8,128)(2,1)S(1)}, bf16[1,1,12,192]{3,2,1,0:T(8,128)(2,1)S(1)}, u32[]{:S(2)}, u32[]{:S(2)}) collective-permute-start(bf16[1,1,12,192]{3,2,1,0:T(8,128)(2,1)S(1)} %get-tuple-element.18), channel_id=1, source_target_pairs={{0,64},{32,96},{64,0},{96,32},{128,192},{160,224},{192,128},{224,1... | collective-permute-start | bytes 13832 | tf_op jit(solution)/shard_map/ppermute | solution.py:86
  12.7 24.8 %collective-permute-start.2 = (bf16[1,1,12,192]{3,2,1,0:T(8,128)(2,1)S(1)}, bf16[1,1,12,192]{3,2,1,0:T(8,128)(2,1)S(1)}, u32[]{:S(2)}, u32[]{:S(2)}) collective-permute-start(bf16[1,1,12,192]{3,2,1,0:T(8,128)(2,1)S(1)} %get-tuple-element.17), channel_id=1, source_target_pairs={{0,96},{32,64},{64,32},{96,0},{128,224},{160,192},{192,160},{224,1... | collective-permute-start | bytes 13832 | tf_op jit(solution)/shard_map/ppermute | solution.py:86
  16.1 32.8 %collective-permute-start.3 = (bf16[1,1,12,192]{3,2,1,0:T(8,128)(2,1)S(1)}, bf16[1,1,12,192]{3,2,1,0:T(8,128)(2,1)S(1)}, u32[]{:S(2)}, u32[]{:S(2)}) collective-permute-start(bf16[1,1,12,192]{3,2,1,0:T(8,128)(2,1)S(1)} %get-tuple-element.16), channel_id=1, source_target_pairs={{0,128},{32,160},{64,192},{96,224},{128,0},{160,32},{192,64},{224,... | collective-permute-start | bytes 13832 | tf_op jit(solution)/shard_map/ppermute | solution.py:86
  22.1 31.5 %collective-permute-start.4 = (bf16[1,1,12,192]{3,2,1,0:T(8,128)(2,1)S(1)}, bf16[1,1,12,192]{3,2,1,0:T(8,128)(2,1)S(1)}, u32[]{:S(2)}, u32[]{:S(2)}) collective-permute-start(bf16[1,1,12,192]{3,2,1,0:T(8,128)(2,1)S(1)} %get-tuple-element.15), channel_id=1, source_target_pairs={{0,160},{32,128},{64,224},{96,192},{128,32},{160,0},{192,96},{224,... | collective-permute-start | bytes 13832 | tf_op jit(solution)/shard_map/ppermute | solution.py:86
  27.4 31.2 %collective-permute-start.5 = (bf16[1,1,12,192]{3,2,1,0:T(8,128)(2,1)S(1)}, bf16[1,1,12,192]{3,2,1,0:T(8,128)(2,1)S(1)}, u32[]{:S(2)}, u32[]{:S(2)}) collective-permute-start(bf16[1,1,12,192]{3,2,1,0:T(8,128)(2,1)S(1)} %get-tuple-element.14), channel_id=1, source_target_pairs={{0,192},{32,224},{64,128},{96,160},{128,64},{160,96},{192,0},{224,... | collective-permute-start | bytes 13832 | tf_op jit(solution)/shard_map/ppermute | solution.py:86
  33.8 31.2 %collective-permute-start.6 = (bf16[1,1,12,192]{3,2,1,0:T(8,128)(2,1)S(1)}, bf16[1,1,12,192]{3,2,1,0:T(8,128)(2,1)S(1)}, u32[]{:S(2)}, u32[]{:S(2)}) collective-permute-start(bf16[1,1,12,192]{3,2,1,0:T(8,128)(2,1)S(1)} %get-tuple-element.13), channel_id=1, source_target_pairs={{0,224},{32,192},{64,160},{96,128},{128,96},{160,64},{192,32},{224... | collective-permute-start | bytes 13832 | tf_op jit(solution)/shard_map/ppermute | solution.py:86
  37.5 32.6 %collective-permute-start.7 = (bf16[1,1,12,192]{3,2,1,0:T(8,128)(2,1)S(1)}, bf16[1,1,12,192]{3,2,1,0:T(8,128)(2,1)S(1)}, u32[]{:S(2)}, u32[]{:S(2)}) collective-permute-start(bf16[1,1,12,192]{3,2,1,0:T(8,128)(2,1)S(1)} %get-tuple-element.12), channel_id=1, source_target_pairs={{0,256},{32,288},{64,320},{96,352},{128,384},{160,416},{192,448},{... | collective-permute-start | bytes 13832 | tf_op jit(solution)/shard_map/ppermute | solution.py:86
  48.9 27.3 %collective-permute-start.8 = (bf16[1,1,12,192]{3,2,1,0:T(8,128)(2,1)S(1)}, bf16[1,1,12,192]{3,2,1,0:T(8,128)(2,1)S(1)}, u32[]{:S(2)}, u32[]{:S(2)}) collective-permute-start(bf16[1,1,12,192]{3,2,1,0:T(8,128)(2,1)S(1)} %get-tuple-element.11), channel_id=1, source_target_pairs={{0,288},{32,256},{64,352},{96,320},{128,416},{160,384},{192,480},{... | collective-permute-start | bytes 13832 | tf_op jit(solution)/shard_map/ppermute | solution.py:86
  53.6 28.2 %collective-permute-start.9 = (bf16[1,1,12,192]{3,2,1,0:T(8,128)(2,1)S(1)}, bf16[1,1,12,192]{3,2,1,0:T(8,128)(2,1)S(1)}, u32[]{:S(2)}, u32[]{:S(2)}) collective-permute-start(bf16[1,1,12,192]{3,2,1,0:T(8,128)(2,1)S(1)} %get-tuple-element.10), channel_id=1, source_target_pairs={{0,320},{32,352},{64,256},{96,288},{128,448},{160,480},{192,384},{... | collective-permute-start | bytes 13832 | tf_op jit(solution)/shard_map/ppermute | solution.py:86
  58.6 26.5 %collective-permute-start.10 = (bf16[1,1,12,192]{3,2,1,0:T(8,128)(2,1)S(1)}, bf16[1,1,12,192]{3,2,1,0:T(8,128)(2,1)S(1)}, u32[]{:S(2)}, u32[]{:S(2)}) collective-permute-start(bf16[1,1,12,192]{3,2,1,0:T(8,128)(2,1)S(1)} %get-tuple-element.9), channel_id=1, source_target_pairs={{0,352},{32,320},{64,288},{96,256},{128,480},{160,448},{192,416},{... | collective-permute-start | bytes 13832 | tf_op jit(solution)/shard_map/ppermute | solution.py:86
  65.0 20.1 %collective-permute-start.11 = (bf16[1,1,12,192]{3,2,1,0:T(8,128)(2,1)S(1)}, bf16[1,1,12,192]{3,2,1,0:T(8,128)(2,1)S(1)}, u32[]{:S(2)}, u32[]{:S(2)}) collective-permute-start(bf16[1,1,12,192]{3,2,1,0:T(8,128)(2,1)S(1)} %get-tuple-element.8), channel_id=1, source_target_pairs={{0,384},{32,416},{64,448},{96,480},{128,256},{160,288},{192,320},{... | collective-permute-start | bytes 13832 | tf_op jit(solution)/shard_map/ppermute | solution.py:86
  70.1 15.1 %collective-permute-start.12 = (bf16[1,1,12,192]{3,2,1,0:T(8,128)(2,1)S(1)}, bf16[1,1,12,192]{3,2,1,0:T(8,128)(2,1)S(1)}, u32[]{:S(2)}, u32[]{:S(2)}) collective-permute-start(bf16[1,1,12,192]{3,2,1,0:T(8,128)(2,1)S(1)} %get-tuple-element.7), channel_id=1, source_target_pairs={{0,416},{32,384},{64,480},{96,448},{128,288},{160,256},{192,352},{... | collective-permute-start | bytes 13832 | tf_op jit(solution)/shard_map/ppermute | solution.py:86
  76.2 9.0 %collective-permute-start.13 = (bf16[1,1,12,192]{3,2,1,0:T(8,128)(2,1)S(1)}, bf16[1,1,12,192]{3,2,1,0:T(8,128)(2,1)S(1)}, u32[]{:S(2)}, u32[]{:S(2)}) collective-permute-start(bf16[1,1,12,192]{3,2,1,0:T(8,128)(2,1)S(1)} %get-tuple-element.6), channel_id=1, source_target_pairs={{0,448},{32,480},{64,384},{96,416},{128,320},{160,352},{192,256},{... | collective-permute-start | bytes 13832 | tf_op jit(solution)/shard_map/ppermute | solution.py:86
  81.8 8.6 %collective-permute-start.14 = (bf16[1,1,12,192]{3,2,1,0:T(8,128)(2,1)S(1)}, bf16[1,1,12,192]{3,2,1,0:T(8,128)(2,1)S(1)}, u32[]{:S(2)}, u32[]{:S(2)}) collective-permute-start(bf16[1,1,12,192]{3,2,1,0:T(8,128)(2,1)S(1)} %get-tuple-element.5), channel_id=1, source_target_pairs={{0,480},{32,448},{64,416},{96,384},{128,352},{160,320},{192,288},{... | collective-permute-start | bytes 13832 | tf_op jit(solution)/shard_map/ppermute | solution.py:86
  93.0 7.6 %copy-start.2 = (bf16[24,192]{1,0:T(8,128)(2,1)S(1)}, bf16[24,192]{1,0:T(8,128)(2,1)}, u32[]{:S(2)}) copy-start(bf16[24,192]{1,0:T(8,128)(2,1)} %param.6) | copy-start | bytes 27652
  93.0 49.3 %all-to-all-start.1 = ((bf16[32,16,1,12,192]{4,1,3,2,0:T(8,128)(2,1)}), bf16[32,16,1,12,192]{4,1,3,2,0:T(8,128)(2,1)}, u32[]{:S(2)}, u32[]{:S(2)}) async-start(bf16[32,16,1,12,192]{4,1,3,2,0:T(8,128)(2,1)} %broadcast_in_dim.64), calls=%async_computation.1 | async-start | bytes 6291456 | tf_op jit(solution)/shard_map/all_to_all | solution.py:22
  142.4 34.7 %all-to-all-start = ((f32[32,1,192]{2,1,0:T(1,128)}), f32[32,1,192]{2,1,0:T(1,128)S(1)}, u32[]{:S(2)}, u32[]{:S(2)}) async-start(f32[32,1,192]{2,1,0:T(1,128)} %reshape.104), calls=%async_computation | async-start | bytes 65536 | tf_op jit(solution)/shard_map/all_to_all | solution.py:22
  151.5 6.3 %copy-start.1 = (bf16[6144,128]{1,0:T(8,128)(2,1)S(1)}, bf16[6144,128]{1,0:T(8,128)(2,1)}, u32[]{:S(2)}) copy-start(bf16[6144,128]{1,0:T(8,128)(2,1)} %param.9) | copy-start | bytes 4718596
  177.0 9.0 %copy-start.3 = (s32[24,2]{0,1:T(2,128)S(1)}, s32[24,2]{0,1:T(2,128)}, u32[]{:S(2)}) copy-start(s32[24,2]{0,1:T(2,128)} %param.7) | copy-start | bytes 580
  177.0 49.4 %all-to-all-start.2 = ((bf16[32,16,1,12,192]{4,1,3,2,0:T(8,128)(2,1)}), bf16[32,16,1,12,192]{4,1,3,2,0:T(8,128)(2,1)}, u32[]{:S(2)}, u32[]{:S(2)}) async-start(bf16[32,16,1,12,192]{4,1,3,2,0:T(8,128)(2,1)} %bitcast.93), calls=%async_computation.2 | async-start | bytes 6291456 | tf_op jit(solution)/shard_map/all_to_all | solution.py:49
  229.6 22.5 %all-to-all-start.3 = ((bf16[16,1,12,192]{3,2,1,0:T(8,128)(2,1)}), bf16[16,1,12,192]{3,2,1,0:T(8,128)(2,1)S(1)}, u32[]{:S(2)}, u32[]{:S(2)}) async-start(bf16[16,1,12,192]{3,2,1,0:T(8,128)(2,1)} %copy.64), calls=%async_computation.3 | async-start | bytes 262144 | tf_op jit(solution)/shard_map/all_to_all | solution.py:99
